TPU v7x, 256 devices: a whole 4x4x8 slice. The times are simulated.
256 devices in a mesh: fsdp: 32 (over x_hi, z, core), tp: 8 (over x_lo, y).
Axes of the slice: x: 4 (x_hi: 2, x_lo: 2; x = x_hi * 2 + x_lo), y: 4, z: 8, core: 2. Of those that a mesh axis runs over, the one named last changes fastest.
Arguments:
- hidden: bfloat16 [2048, 26624], P('fsdp', 'tp'), may hold values from -6 to 6
- out_grad: bfloat16 [2048, 16384], P('tp', 'fsdp'), may hold values from -6 to 6
- weight: bfloat16 [26624, 16384], P('tp', 'fsdp'), may hold values from -0.0390625 to 0.0390625
Outputs:
- hidden_grad: bfloat16 [2048, 26624], P('fsdp', 'tp')
- weight_grad: float32 [26624, 16384], P('tp', 'fsdp')
All inputs are finite; a program needn't handle non-finite values.
Results may differ from a plain program's by a relative error of at most 0.015.
Values may be sent and summed in bfloat16 or wider, within the bound.
No kernel may reach another device: no remote copies, remote signals or barrier semaphores. Data moves between devices by JAX's collectives and lax.ppermute only.
A program may use at most 128 MiB of HBM per device.

v0:
```python
import math
import jax
import jax.numpy as jnp
from jax import lax
from jax.sharding import PartitionSpec as P


def local(hidden, out_grad, weight):
    grad_rows = lax.all_gather(out_grad, "tp", axis=0, tiled=True)
    partial_sum = lax.dot_general(
        grad_rows, weight, (((1,), (1,)), ((), ())), preferred_element_type=jnp.float32
    )
    adjoint = lax.psum_scatter(
        partial_sum.astype(jnp.bfloat16), "fsdp", scatter_dimension=0, tiled=True
    ).astype(jnp.float32)
    hidden_grad = (adjoint + 0.5 * hidden.astype(jnp.float32)).astype(jnp.bfloat16)
    all_hidden = lax.all_gather(hidden, "fsdp", axis=0, tiled=True)
    weight_grad = lax.dot_general(
        all_hidden, grad_rows, (((0,), (0,)), ((), ())), preferred_element_type=jnp.float32
    )
    grad_scale = 1.0 / math.sqrt(grad_rows.shape[0])
    return (hidden_grad, weight_grad * grad_scale)


def solution(mesh):
    placed = (P("fsdp", "tp"), P("tp", "fsdp"), P("tp", "fsdp"))
    return jax.shard_map(
        local,
        mesh=mesh,
        in_specs=placed,
        out_specs=(P("fsdp", "tp"), P("tp", "fsdp")),
        check_vma=False,
    )
```

profile of v0, /device:TPU:1, one launch (start us, length us, event | category | flops | bytes accessed | tf_op | source)
XLA Modules:
  0.0 391.0 jit_solution(8042441853930988488)
XLA Ops:
  7.2 0.0 copy-start
  7.2 0.0 all-gather.3.cloned.1.call-start
  7.2 0.7 all-gather.3.cloned.1.call-update
  7.9 0.0 reduce-scatter.2.cloned.1.call-start
  8.0 44.1 %all-gather.3.cloned.1.call-done = bf16[2048,512]{1,0:T(8,128)(2,1)} async-done(((bf16[256,512]{1,0:T(8,128)(2,1)}), bf16[2048,512]{1,0:T(8,128)(2,1)}) %all-gather.3.cloned.1.call-update) | async-done | bytes 2097168 | tf_op jit(solution)/shard_map/all_gather | solution.py:9
  52.0 0.0 copy-done
  52.0 12.5 %convolution_convert_fusion = bf16[2048,3328]{1,0:T(8,128)(2,1)} fusion(bf16[2048,512]{1,0:T(8,128)(2,1)} %all-gather.3.cloned.1.call-done, bf16[3328,512]{1,0:T(8,128)(2,1)S(1)} %copy-done), kind=kOutput, calls=%fused_computation | convolution fusion | flops 6986137600 | bytes 19136512 | tf_op jit(solution)/shard_map/dot_general | solution.py:10
  64.5 0.0 reduce-scatter.2.cloned.1.call-update
  64.5 0.0 all-gather.5.cloned.1.call-start
  64.6 0.7 all-gather.5.cloned.1.call-update
  65.3 178.9 %reduce-scatter.2.cloned.1.call-done = bf16[64,3328]{1,0:T(8,128)(2,1)} async-done(((bf16[2048,3328]{1,0:T(8,128)(2,1)}), bf16[64,3328]{1,0:T(8,128)(2,1)}) %reduce-scatter.2.cloned.1.call-update) | async-done | bytes 426000 | tf_op jit(solution)/shard_map/reduce_scatter | solution.py:13
  244.2 2.0 add_convert_fusion
  246.2 125.5 %all-gather.5.cloned.1.call-done = bf16[2048,3328]{1,0:T(8,128)(2,1)} async-done(((bf16[64,3328]{1,0:T(8,128)(2,1)}), bf16[2048,3328]{1,0:T(8,128)(2,1)}) %all-gather.5.cloned.1.call-update) | async-done | bytes 13631504 | tf_op jit(solution)/shard_map/all_gather | solution.py:17
  371.7 12.8 %convolution_multiply_fusion = f32[3328,512]{1,0:T(8,128)} fusion(bf16[2048,3328]{1,0:T(8,128)(2,1)} %all-gather.5.cloned.1.call-done, bf16[2048,512]{1,0:T(8,128)(2,1)} %all-gather.3.cloned.1.call-done), kind=kOutput, calls=%fused_computation.1 | convolution fusion | flops 6981025792 | bytes 22544384 | tf_op jit(solution)/shard_map/dot_general | solution.py:18
Async XLA Ops:
  7.2 44.9 %copy-start = (bf16[3328,512]{1,0:T(8,128)(2,1)S(1)}, bf16[3328,512]{1,0:T(8,128)(2,1)}, u32[]{:S(2)}) copy-start(bf16[3328,512]{1,0:T(8,128)(2,1)} %param.5) | copy-start | bytes 10223620
  7.2 44.9 %all-gather.3.cloned.1.call-start = ((), (), s32[]{:S(2)}) async-start(), calls=%async_computation.1 | async-start | bytes 2359296 | tf_op jit(solution)/shard_map/all_gather | solution.py:9
  7.9 236.2 %reduce-scatter.2.cloned.1.call-start = ((), (), s32[]{:S(2)}) async-start(), calls=%async_computation.2 | async-start | bytes 14057472 | tf_op jit(solution)/shard_map/reduce_scatter | solution.py:13
  64.5 307.1 %all-gather.5.cloned.1.call-start = ((), (), s32[]{:S(2)}) async-start(), calls=%async_computation.3 | async-start | bytes 14057472 | tf_op jit(solution)/shard_map/all_gather | solution.py:17
Sparse Core Ops, SparseCore 0:
  9.8 42.2 all-gather.2
  64.7 179.4 reduce-scatter.1
  246.9 124.6 all-gather.4
where the time goes:
time: 391 us
  waiting for transfers between devices  350 us (90%)
  matrix products  25.2 us (6%)
  between operations  13.8 us (4%)
    reduce_scatter x1, waiting for transfers between devices, local(): lax.psum_scatter(partial_sum.astype(jnp.bfloat16), 'fsdp', scatter_dimens...  179 us
    all_gather x1, waiting for transfers between devices, local(): all_hidden = lax.all_gather(hidden, 'fsdp', axis=0, tiled=True)  125 us
    all_gather x1, waiting for transfers between devices, local(): grad_rows = lax.all_gather(out_grad, 'tp', axis=0, tiled=True)  44.1 us
    dot_general x1, matrix products, local(): lax.dot_general(all_hidden, grad_rows, (((0,), (0,)), ((), ())), preferre...  12.8 us
    dot_general x1, matrix products, local(): lax.dot_general(grad_rows, weight, (((1,), (1,)), ((), ())), preferred_el...  12.5 us
  transfers between devices with their start and end apart: 3, of which 3 were waited for; matrix products, arithmetic and copies ran while one was open for 1% of the time, Pallas kernels for 0%

commit v1 on v0

--- a/solution.py
+++ b/solution.py
@@ -6,7 +6,9 @@
 
 
 def local(hidden, out_grad, weight):
-    grad_rows = lax.all_gather(out_grad, "tp", axis=0, tiled=True)
+    grad_rows = jnp.concatenate(
+        lax.all_to_all(jnp.stack([out_grad] * lax.axis_size("tp")), "tp", 0, 0), axis=0
+    )
     partial_sum = lax.dot_general(
         grad_rows, weight, (((1,), (1,)), ((), ())), preferred_element_type=jnp.float32
     )

time: 391 us -> 376 us (0.962)
  waiting for transfers between devices: 350 us -> 302 us
  blocking collectives: 0 us -> 31.5 us
    all_gather x1 -> x0, waiting for transfers between devices: 44.1 us -> none  [local(): grad_rows = lax.all_gather(out_grad, 'tp', axis=0, tiled=True)]
    all_to_all x0 -> x1, blocking collectives: none -> 31.5 us  [local(): lax.all_to_all(jnp.stack([out_grad] * lax.axis_size('tp')), 'tp', 0, 0)]
  transfers between devices with their start and end apart: 3 -> 2, of which waited for: 3 -> 2; matrix products, arithmetic and copies ran while one was open for 1% -> 1% of each run, Pallas kernels for 0% -> 0%
where the time goes in v1:
time: 376 us
  waiting for transfers between devices  302 us (80%)
  blocking collectives  31.5 us (8%)
  matrix products  23.2 us (6%)
  between operations  14.1 us (4%)
    reduce_scatter x1, waiting for transfers between devices, local(): lax.psum_scatter(partial_sum.astype(jnp.bfloat16), 'fsdp', scatter_dimens...  176 us
    all_gather x1, waiting for transfers between devices, local(): all_hidden = lax.all_gather(hidden, 'fsdp', axis=0, tiled=True)  125 us
    all_to_all x1, blocking collectives, local(): lax.all_to_all(jnp.stack([out_grad] * lax.axis_size('tp')), 'tp', 0, 0)  31.5 us
    dot_general x1, matrix products, local(): lax.dot_general(all_hidden, grad_rows, (((0,), (0,)), ((), ())), preferre...  12.8 us
    dot_general x1, matrix products, local(): lax.dot_general(grad_rows, weight, (((1,), (1,)), ((), ())), preferred_el...  10.4 us
  transfers between devices with their start and end apart: 2, of which 2 were waited for; matrix products, arithmetic and copies ran while one was open for 1% of the time, Pallas kernels for 0%

profile of v1, /device:TPU:1, one launch (start us, length us, event | category | flops | bytes accessed | tf_op | source)
XLA Modules:
  0.0 375.8 jit_solution(5507746861522302673)
XLA Ops:
  7.2 0.0 copy-start
  7.2 0.0 reduce-scatter.2.cloned.1.call-start
  7.2 1.3 stack.2
  8.5 31.5 %all_to_all.5 = bf16[8,256,512]{2,1,0:T(8,128)(2,1)S(1)} all-to-all(bf16[8,256,512]{2,1,0:T(8,128)(2,1)S(1)} %stack.2), channel_id=1, replica_groups=mesh['fsdp'=32,'tp'=8] {'tp'}, dimensions={0} | all-to-all | bytes 4194304 | tf_op jit(solution)/shard_map/all_to_all | solution.py:10
  40.0 0.0 copy-start.1
  40.0 1.3 copy-done.1
  41.3 0.0 copy-done
  41.3 10.4 %convolution_convert_fusion = bf16[2048,3328]{1,0:T(8,128)(2,1)} fusion(bf16[2048,512]{1,0:T(8,128)(2,1)S(1)} %bitcast.5, bf16[3328,512]{1,0:T(8,128)(2,1)S(1)} %copy-done), kind=kOutput, calls=%fused_computation | convolution fusion | flops 6986137600 | bytes 19136512 | tf_op jit(solution)/shard_map/dot_general | solution.py:12
  51.7 0.0 reduce-scatter.2.cloned.1.call-update
  51.7 0.0 all-gather.2.cloned.1.call-start
  51.7 0.7 all-gather.2.cloned.1.call-update
  52.4 176.3 %reduce-scatter.2.cloned.1.call-done = bf16[64,3328]{1,0:T(8,128)(2,1)} async-done(((bf16[2048,3328]{1,0:T(8,128)(2,1)}), bf16[64,3328]{1,0:T(8,128)(2,1)}) %reduce-scatter.2.cloned.1.call-update) | async-done | bytes 426000 | tf_op jit(solution)/shard_map/reduce_scatter | solution.py:15
  228.7 2.0 add_convert_fusion
  230.8 125.3 %all-gather.2.cloned.1.call-done = bf16[2048,3328]{1,0:T(8,128)(2,1)} async-done(((bf16[64,3328]{1,0:T(8,128)(2,1)}), bf16[2048,3328]{1,0:T(8,128)(2,1)}) %all-gather.2.cloned.1.call-update) | async-done | bytes 13631504 | tf_op jit(solution)/shard_map/all_gather | solution.py:19
  356.1 12.8 %convolution_multiply_fusion = f32[3328,512]{1,0:T(8,128)} fusion(bf16[2048,3328]{1,0:T(8,128)(2,1)} %all-gather.2.cloned.1.call-done, bf16[2048,512]{1,0:T(8,128)(2,1)} %bitcast.6), kind=kOutput, calls=%fused_computation.1 | convolution fusion | flops 6981025792 | bytes 22544384 | tf_op jit(solution)/shard_map/dot_general | solution.py:20
Async XLA Ops:
  7.2 34.1 %copy-start = (bf16[3328,512]{1,0:T(8,128)(2,1)S(1)}, bf16[3328,512]{1,0:T(8,128)(2,1)}, u32[]{:S(2)}) copy-start(bf16[3328,512]{1,0:T(8,128)(2,1)} %param.5) | copy-start | bytes 10223620
  7.2 221.6 %reduce-scatter.2.cloned.1.call-start = ((), (), s32[]{:S(2)}) async-start(), calls=%async_computation.2 | async-start | bytes 14057472 | tf_op jit(solution)/shard_map/reduce_scatter | solution.py:15
  40.0 1.3 copy-start.1
  51.7 304.4 %all-gather.2.cloned.1.call-start = ((), (), s32[]{:S(2)}) async-start(), calls=%async_computation.3 | async-start | bytes 14057472 | tf_op jit(solution)/shard_map/all_gather | solution.py:19
Sparse Core Ops, SparseCore 0:
  51.8 176.8 reduce-scatter.1
  231.5 124.5 all-gather.1
